TPU v7x, 128 devices: a whole 4x4x4 slice. The times are simulated.
128 devices in a mesh: tier: 8 (over y, z_lo), tile: 16 (over x, z_hi, core).
Axes of the slice: x: 4, y: 4, z: 4 (z_hi: 2, z_lo: 2; z = z_hi * 2 + z_lo), core: 2. Of those that a mesh axis runs over, the one named last changes fastest.
Arguments:
- warming_above_ambient: float32 [8, 16, 512, 2048], P('tier', None, 'tile'), may hold values from -6 to 6
- substance_label: int32 [8, 16, 512, 2048], P('tier', None, 'tile'), may hold values from 0 to 15
- glue_zone_label: int32 [512, 2048], P('tile'), may hold values from 0 to 7
- patch_label_per_cell: int32 [8, 512, 2048], P('tier', 'tile'), may hold values from 0 to 127
- heat_conductance_per_substance: float32 [16], replicated, may hold values from 0.3 to 4
- dissipation_per_patch: float32 [8, 128], P('tier'), may hold values from 0.5 to 5
- glue_sheet_reciprocal_operators: float32 [8, 16, 16], replicated, may hold values from -0.3 to 1.3, as said below
Outputs:
- final_state: float32 [8, 16, 512, 2048], P('tier', None, 'tile')
Inputs may be any that keep to these rules, and one draw needn't show every extreme that they name: `glue_sheet_reciprocal_operators`: each matrix has diagonal entries of 0.6 to 1.0 plus a perturbation, and perturbed entries elsewhere.
All inputs are finite; a program needn't handle non-finite values.
Results may differ from a plain program's by a relative error of at most 0.0001.
Values sent between devices are 32-bit elements; how exact they have to be, the bound alone decides.
A program may use at most 128 MiB of HBM per device.

v0:
```python
import jax
import jax.numpy as jnp
from jax import lax
from jax.sharding import PartitionSpec as P

MATERIALS = 16
REGIONS = 8
POWER_TILES = 128
STEPS = 2
step_dt = 0.04


def padded(cells, sides, width):
    for axis, dim in sides:
        count = lax.axis_size(axis)
        ends = count - 1
        head = lax.slice_in_dim(cells, 0, width, axis=dim)
        tail = lax.slice_in_dim(cells, cells.shape[dim] - width, cells.shape[dim], axis=dim)
        cells = jnp.concatenate(
            [
                lax.ppermute(tail, axis, [(i, (i + 1) % count) for i in range(ends)]),
                cells,
                lax.ppermute(head, axis, [((i + 1) % count, i) for i in range(ends)]),
            ],
            axis=dim,
        )
    return cells


def pad_axis(field, axis, low, high):
    widths = [(0, 0)] * field.ndim
    widths[axis] = (low, high)
    return jnp.pad(field, widths)


def conduct(padded_t, padded_k):
    centre = padded_t[..., 1:-1, :]
    kcell = padded_k[..., 1:-1, :]
    flux = 0.5 * (kcell + padded_k[..., 2:, :]) * (padded_t[..., 2:, :] - centre)
    flux = flux + 0.5 * (kcell + padded_k[..., :-2, :]) * (padded_t[..., :-2, :] - centre)
    side_t = pad_axis(centre, centre.ndim - 1, 1, 1)
    side_k = pad_axis(kcell, kcell.ndim - 1, 1, 1)
    flux = flux + 0.5 * (kcell + side_k[..., 2:]) * (side_t[..., 2:] - centre)
    flux = flux + 0.5 * (kcell + side_k[..., :-2]) * (side_t[..., :-2] - centre)
    face = (
        0.5
        * (kcell[..., 1:, :, :] + kcell[..., :-1, :, :])
        * (centre[..., 1:, :, :] - centre[..., :-1, :, :])
    )
    axis = centre.ndim - 3
    return flux + pad_axis(face, axis, 0, 1) - pad_axis(face, axis, 1, 0)


def select_solve(matrices, planes, regions):
    solved = jnp.zeros((matrices.shape[1],) + planes.shape[1:], jnp.float32)
    for which in range(REGIONS):
        mapped = jnp.einsum("ij,jxc->ixc", matrices[which], planes, precision=lax.Precision.HIGHEST)
        solved = solved + jnp.where(regions == which, mapped, 0.0)
    return solved


def local(
    warming_above_ambient,
    substance_label,
    glue_zone_label,
    patch_label_per_cell,
    heat_conductance_per_substance,
    dissipation_per_patch,
    glue_sheet_reciprocal_operators,
):
    kappa = jnp.zeros(substance_label.shape, jnp.float32)
    for which in range(MATERIALS):
        kappa = jnp.where(substance_label == which, heat_conductance_per_substance[which], kappa)
    onehot = (patch_label_per_cell[0][..., None] == lax.iota(jnp.int32, POWER_TILES)).astype(
        jnp.float32
    )
    source = jnp.dot(
        onehot.reshape(-1, POWER_TILES), dissipation_per_patch[0], precision=lax.Precision.HIGHEST
    )
    source = source.reshape(patch_label_per_cell.shape[1:])
    tier_index = lax.axis_index("tier")
    heating_snapshot = warming_above_ambient
    for step in range(STEPS):
        joined = padded(jnp.stack([heating_snapshot, kappa]), (("tile", 3),), 1)
        padded_t = joined[0]
        padded_k = joined[1]
        heating_snapshot = heating_snapshot + step_dt * conduct(padded_t, padded_k)
        heating_snapshot = heating_snapshot.at[:, 0].add(step_dt * source)
        planes = jnp.stack([heating_snapshot[0, 0], heating_snapshot[0, -1]])
        gathered = lax.all_gather(planes, "tier", axis=0, tiled=True)
        own_rows = lax.dynamic_slice_in_dim(glue_sheet_reciprocal_operators, 2 * tier_index, 2, 1)
        updated = select_solve(own_rows, gathered, glue_zone_label)
        heating_snapshot = heating_snapshot.at[0, 0].set(updated[0]).at[0, -1].set(updated[1])
    return heating_snapshot


def solution(mesh):
    in_specs = (
        P("tier", None, "tile", None),
        P("tier", None, "tile", None),
        P("tile", None),
        P("tier", "tile", None),
        P(),
        P("tier", None),
        P(),
    )
    out_specs = P("tier", None, "tile", None)
    return jax.shard_map(local, mesh=mesh, in_specs=in_specs, out_specs=out_specs, check_vma=False)
```

profile of v0, /device:TPU:27, one launch (start us, length us, event | category | flops | bytes accessed | tf_op | source)
XLA Modules:
  0.0 563.4 jit_solution(4008973471089859055)
XLA Ops:
  8.5 5.0 stack.22
  13.5 44.8 %fusion.8 = f32[1,1,16,32,2048]{4,0,3,2,1:T(1,128)S(1)} fusion(s32[1,16,32,2048]{3,2,1,0:T(8,128)S(1)} %copy-done.16, f32[]{:T(128)} %bitcast.15, f32[]{:T(128)} %bitcast.14, f32[]{:T(128)} %bitcast.13, f32[]{:T(128)} %bitcast.12, f32[]{:T(128)} %bitcast.11, f32[]{:T(128)} %bitcast.10, f32[]{:T(128)} %bitcast.9, f32[]{:T(128)} %bitcast.8, f32[]{:T(128)} %bitcast.7, ...), kind=kLoop, calls=%fused_computation.33 | loop fusion | flops 33554432 | bytes 8388672 | tf_op jit(solution)/shard_map/stack | solution.py:84
  58.9 6.1 %collective-permute-start = (f32[2,1,16,1,2048]{4,0,3,2,1:T(2,128)S(1)}, f32[2,1,16,1,2048]{4,0,3,2,1:T(2,128)S(1)}, u32[]{:S(2)}, u32[]{:S(2)}) collective-permute-start(f32[2,1,16,1,2048]{4,0,3,2,1:T(2,128)S(1)} %get-tuple-element.77), channel_id=1, source_target_pairs={{0,1},{1,2},{2,3},{3,4},{4,5},{5,6},{6,7},{7,8},{8,9},{9,10},{10,1... | collective-permute-start | bytes 786440 | tf_op jit(solution)/shard_map/ppermute | solution.py:21
  67.1 23.6 %fusion.1 = f32[1,32,2048]{2,0,1:T(1,128)S(1)} fusion(s32[32,2048]{1,0:T(8,128)S(1)} %bitcast.110, f32[1,128]{1,0:T(1,128)S(1)} %copy-done.20), kind=kOutput, calls=%fused_computation.2 | convolution fusion | flops 109051904 | bytes 524800 | tf_op jit(solution)/shard_map/dot_general | solution.py:77
  90.8 8.0 %fusion.5 = f32[2,1,16,34,2048]{4,0,3,2,1:T(2,128)S(1)} fusion(f32[1,1,16,32,2048]{4,0,3,2,1:T(1,128)S(1)} %fusion.8, f32[2,1,16,1,2048]{4,0,3,2,1:T(2,128)S(1)} %collective-permute-done.1, f32[1,1,16,32,2048]{4,0,3,2,1:T(1,128)S(1)} %stack.22, f32[2,1,16,1,2048]{4,0,3,2,1:T(2,128)S(1)} %collective-permute-done), kind=kLoop, calls=%fused_computation.23 | loop fusion | flops 6684672 | bytes 17825792 | tf_op jit(solution)/shard_map/concatenate | solution.py:19
  98.8 7.9 %slice_bitcast_fusion.3 = (f32[1,16,34,2048]{3,0,2,1:T(1,128)S(1)}, f32[1,16,34,2048]{3,0,2,1:T(1,128)}) fusion(f32[2,1,16,34,2048]{4,0,3,2,1:T(2,128)S(1)} %fusion.5), kind=kLoop, calls=%fused_computation.32 | loop fusion | bytes 17825792 | tf_op jit(solution)/shard_map/squeeze | solution.py:86
  106.7 5.2 slice.452
  111.9 7.9 %slice.456 = f32[1,16,32,2048]{3,0,2,1:T(1,128)} slice(f32[1,16,34,2048]{3,0,2,1:T(1,128)} %get-tuple-element.84), slice={[0:1], [0:16], [1:33], [0:2048]} | slice | bytes 8388608 | tf_op jit(solution)/shard_map/slice | solution.py:37
  119.8 11.4 %fusion.21 = f32[1,15,32,2048]{3,0,2,1:T(1,128)S(1)} fusion(f32[1,16,34,2048]{3,0,2,1:T(1,128)} %get-tuple-element.84, f32[1,16,34,2048]{3,0,2,1:T(1,128)S(1)} %get-tuple-element.83), kind=kLoop, calls=%fused_computation.59 | loop fusion | flops 3932160 | bytes 19660800 | tf_op jit(solution)/shard_map/mul | solution.py:46
  131.2 46.0 %copy_add_fusion = f32[1,16,32,2048]{3,0,2,1:T(1,128)S(1)} fusion(f32[1,16,32,2048]{3,2,1,0:T(8,128)S(1)} %copy-done.11, f32[1,15,32,2048]{3,0,2,1:T(1,128)S(1)} %fusion.21, f32[1,16,32,2048]{3,0,2,1:T(1,128)S(1)} %copy-done.15, f32[1,16,32,2048]{3,0,2,1:T(1,128)S(1)} %copy-done.13, f32[1,16,34,2048]{3,0,2,1:T(1,128)} %get-tuple-element.84, ...), kind=kLoop, calls=%fused_computation.52 | loop fusion | flops 24117248 | bytes 37486592 | tf_op jit(solution)/shard_map/add | solution.py:87
  183.5 90.0 %all-gather.3.cloned.1.call-done = f32[16,32,2048]{2,1,0:T(8,128)} async-done(((f32[2,32,2048]{2,1,0:T(8,128)}), f32[16,32,2048]{2,1,0:T(8,128)}) %all-gather.3.cloned.1.call-update) | async-done | bytes 4194320 | tf_op jit(solution)/shard_map/all_gather | solution.py:90
  273.5 6.8 %fusion.55 = f32[2,32,2048]{2,0,1:T(2,128)S(1)} fusion(f32[16,32,2048]{2,1,0:T(8,128)} %all-gather.3.cloned.1.call-done, pred[32,2048]{1,0:T(8,128)(4,1)S(1)} %get-tuple-element.99, f32[8,16,16]{2,1,0:T(8,128)S(1)} %copy-done, s32[]{:T(128)S(6)} %select_n.118), kind=kOutput, calls=%fused_computation.94 | convolution fusion | flops 25296896 | bytes 4785156 | tf_op jit(solution)/shard_map/ij,jxc->ixc/dot_general | solution.py:57
  294.6 5.1 fusion.133
  324.2 5.9 %collective-permute-done.3 = f32[2,1,16,1,2048]{4,0,3,2,1:T(2,128)S(1)} collective-permute-done((f32[2,1,16,1,2048]{4,0,3,2,1:T(2,128)S(1)}, f32[2,1,16,1,2048]{4,0,3,2,1:T(2,128)S(1)}, u32[]{:S(2)}, u32[]{:S(2)}) %collective-permute-start.3) | collective-permute-done | bytes 262176 | tf_op jit(solution)/shard_map/ppermute | solution.py:23
  330.1 8.1 %fusion.7 = f32[2,1,16,34,2048]{4,0,3,2,1:T(2,128)S(1)} fusion(f32[1,1,16,32,2048]{4,0,3,2,1:T(1,128)S(1)} %copy-done.8, f32[2,1,16,1,2048]{4,0,3,2,1:T(2,128)S(1)} %collective-permute-done.3, f32[1,1,16,32,2048]{4,0,3,2,1:T(1,128)S(1)} %bitcast.109, f32[2,1,16,1,2048]{4,0,3,2,1:T(2,128)S(1)} %collective-permute-done.2), kind=kLoop, calls=%fused_computation.25 | loop fusion | flops 6684672 | bytes 17825792 | tf_op jit(solution)/shard_map/concatenate | solution.py:19
  338.2 7.9 %slice_bitcast_fusion.1 = (f32[1,16,34,2048]{3,0,2,1:T(1,128)S(1)}, f32[1,16,34,2048]{3,0,2,1:T(1,128)}) fusion(f32[2,1,16,34,2048]{4,0,3,2,1:T(2,128)S(1)} %fusion.7), kind=kLoop, calls=%fused_computation.30 | loop fusion | bytes 17825792 | tf_op jit(solution)/shard_map/squeeze | solution.py:86
  346.1 5.2 slice.470
  351.3 7.9 %slice.474 = f32[1,16,32,2048]{3,0,2,1:T(1,128)} slice(f32[1,16,34,2048]{3,0,2,1:T(1,128)} %get-tuple-element.82), slice={[0:1], [0:16], [1:33], [0:2048]} | slice | bytes 8388608 | tf_op jit(solution)/shard_map/slice | solution.py:37
  359.2 11.4 %fusion.19 = f32[1,15,32,2048]{3,0,2,1:T(1,128)S(1)} fusion(f32[1,16,34,2048]{3,0,2,1:T(1,128)} %get-tuple-element.82, f32[1,16,34,2048]{3,0,2,1:T(1,128)S(1)} %get-tuple-element.81), kind=kLoop, calls=%fused_computation.55 | loop fusion | flops 3932160 | bytes 19660800 | tf_op jit(solution)/shard_map/mul | solution.py:46
  370.6 42.8 %multiply_add_fusion = f32[1,16,32,2048]{3,0,2,1:T(1,128)S(1)} fusion(f32[1,16,32,2048]{3,0,2,1:T(1,128)S(1)} %copy-done.6, f32[1,15,32,2048]{3,0,2,1:T(1,128)S(1)} %fusion.19, f32[1,16,32,2048]{3,0,2,1:T(1,128)S(1)} %copy-done.14, f32[1,16,32,2048]{3,0,2,1:T(1,128)S(1)} %copy-done.12, f32[1,16,34,2048]{3,0,2,1:T(1,128)} %get-tuple-element.82, ...), kind=kLoop, calls=%fused_computation.53 | loop fusion | flops 24117248 | bytes 37486592 | tf_op jit(solution)/shard_map/add | solution.py:87
  417.5 92.2 %all-gather.5.cloned.1.call-done = f32[16,32,2048]{2,1,0:T(8,128)} async-done(((f32[2,32,2048]{2,1,0:T(8,128)}), f32[16,32,2048]{2,1,0:T(8,128)}) %all-gather.5.cloned.1.call-update) | async-done | bytes 4194320 | tf_op jit(solution)/shard_map/all_gather | solution.py:90
  509.7 6.8 %fusion.79 = f32[2,32,2048]{2,0,1:T(2,128)S(1)} fusion(f32[16,32,2048]{2,1,0:T(8,128)} %all-gather.5.cloned.1.call-done, pred[32,2048]{1,0:T(8,128)(4,1)S(1)} %get-tuple-element.99, f32[8,16,16]{2,1,0:T(8,128)S(1)} %copy-done, s32[]{:T(128)S(6)} %select_n.118), kind=kOutput, calls=%fused_computation.102 | convolution fusion | flops 25296896 | bytes 4785156 | tf_op jit(solution)/shard_map/ij,jxc->ixc/dot_general | solution.py:57
  530.9 5.0 fusion.112
  545.3 5.0 fusion.103
  (84 shorter events, 83.4 us)
Async XLA Ops:
  6.5 266.9 %copy-start = (f32[8,16,16]{2,1,0:T(8,128)S(1)}, f32[8,16,16]{2,1,0:T(8,128)}, u32[]{:S(2)}) copy-start(f32[8,16,16]{2,1,0:T(8,128)} %param.25) | copy-start | bytes 24580
  6.5 266.9 %all-gather.3.cloned.1.call-start = ((), (), s32[]{:S(2)}) async-start(), calls=%async_computation | async-start | bytes 4718592 | tf_op jit(solution)/shard_map/all_gather | solution.py:90
  58.3 32.5 %copy-start.7 = (f32[1,1,16,32,2048]{4,0,3,2,1:T(1,128)}, f32[1,1,16,32,2048]{4,0,3,2,1:T(1,128)S(1)}, u32[]{:S(2)}) copy-start(f32[1,1,16,32,2048]{4,0,3,2,1:T(1,128)S(1)} %fusion.8) | copy-start | bytes 12582916
  58.3 8.8 %copy-start.19 = (s32[1,32,2048]{2,1,0:T(8,128)S(1)}, s32[1,32,2048]{2,1,0:T(8,128)}, u32[]{:S(2)}) copy-start(s32[1,32,2048]{2,1,0:T(8,128)} %param.22) | copy-start | bytes 786436
  58.3 8.8 %copy-start.20 = (f32[1,128]{1,0:T(1,128)S(1)}, f32[1,128]{1,0:T(1,128)}, u32[]{:S(2)}) copy-start(f32[1,128]{1,0:T(1,128)} %param.24) | copy-start | bytes 1540
  58.9 31.9 %collective-permute-start = (f32[2,1,16,1,2048]{4,0,3,2,1:T(2,128)S(1)}, f32[2,1,16,1,2048]{4,0,3,2,1:T(2,128)S(1)}, u32[]{:S(2)}, u32[]{:S(2)}) collective-permute-start(f32[2,1,16,1,2048]{4,0,3,2,1:T(2,128)S(1)} %get-tuple-element.77), channel_id=1, source_target_pairs={{0,1},{1,2},{2,3},{3,4},{4,5},{5,6},{6,7},{7,8},{8,9},{9,10},{10,1... | collective-permute-start | bytes 786440 | tf_op jit(solution)/shard_map/ppermute | solution.py:21
  65.0 25.8 %collective-permute-start.1 = (f32[2,1,16,1,2048]{4,0,3,2,1:T(2,128)S(1)}, f32[2,1,16,1,2048]{4,0,3,2,1:T(2,128)S(1)}, u32[]{:S(2)}, u32[]{:S(2)}) collective-permute-start(f32[2,1,16,1,2048]{4,0,3,2,1:T(2,128)S(1)} %get-tuple-element.91), channel_id=1, source_target_pairs={{1,0},{2,1},{3,2},{4,3},{5,4},{6,5},{7,6},{8,7},{9,8},{10,9},{11,1... | collective-permute-start | bytes 786440 | tf_op jit(solution)/shard_map/ppermute | solution.py:23
  119.7 11.4 %copy-start.11 = (f32[1,16,32,2048]{3,2,1,0:T(8,128)S(1)}, f32[1,16,32,2048]{3,2,1,0:T(8,128)}, u32[]{:S(2)}) copy-start(f32[1,16,32,2048]{3,2,1,0:T(8,128)} %param.19) | copy-start | bytes 12582916
  119.7 11.4 %copy-start.13 = (f32[1,16,32,2048]{3,0,2,1:T(1,128)S(1)}, f32[1,16,32,2048]{3,0,2,1:T(1,128)}, u32[]{:S(2)}) copy-start(f32[1,16,32,2048]{3,0,2,1:T(1,128)} %slice.452) | copy-start | bytes 12582916
  119.7 11.4 %copy-start.15 = (f32[1,16,32,2048]{3,0,2,1:T(1,128)S(1)}, f32[1,16,32,2048]{3,0,2,1:T(1,128)}, u32[]{:S(2)}) copy-start(f32[1,16,32,2048]{3,0,2,1:T(1,128)} %slice.456) | copy-start | bytes 12582916
  177.2 5.2 copy-start.18
  177.2 5.9 %copy-start.17 = (s32[32,2048]{1,0:T(8,128)S(1)}, s32[32,2048]{1,0:T(8,128)}, u32[]{:S(2)}) copy-start(s32[32,2048]{1,0:T(8,128)} %param.21) | copy-start | bytes 786436
  181.3 328.4 %all-gather.5.cloned.1.call-start = ((), (), s32[]{:S(2)}) async-start(), calls=%async_computation.1 | async-start | bytes 4718592 | tf_op jit(solution)/shard_map/all_gather | solution.py:90
  273.5 6.8 %copy-start.1 = (f32[16,32,2048]{2,1,0:T(8,128)S(1)}, f32[16,32,2048]{2,1,0:T(8,128)}, u32[]{:S(2)}) copy-start(f32[16,32,2048]{2,1,0:T(8,128)} %all-gather.3.cloned.1.call-done) | copy-start | bytes 12582916
  304.5 9.7 %copy-start.4 = (f32[1,16,32,2048]{3,0,2,1:T(1,128)S(1)}, f32[1,16,32,2048]{3,0,2,1:T(1,128)}, u32[]{:S(2)}) copy-start(f32[1,16,32,2048]{3,0,2,1:T(1,128)} %copy-done.3) | copy-start | bytes 12582916
  314.2 15.8 %copy-start.8 = (f32[1,1,16,32,2048]{4,0,3,2,1:T(1,128)S(1)}, f32[1,1,16,32,2048]{4,0,3,2,1:T(1,128)}, u32[]{:S(2)}) copy-start(f32[1,1,16,32,2048]{4,0,3,2,1:T(1,128)} %copy-done.7) | copy-start | bytes 12582916
  316.5 29.5 %copy-start.5 = (f32[1,16,32,2048]{3,0,2,1:T(1,128)}, f32[1,16,32,2048]{3,0,2,1:T(1,128)S(1)}, u32[]{:S(2)}) copy-start(f32[1,16,32,2048]{3,0,2,1:T(1,128)S(1)} %fusion.147) | copy-start | bytes 12582916
  316.9 7.2 %collective-permute-start.2 = (f32[2,1,16,1,2048]{4,0,3,2,1:T(2,128)S(1)}, f32[2,1,16,1,2048]{4,0,3,2,1:T(2,128)S(1)}, u32[]{:S(2)}, u32[]{:S(2)}) collective-permute-start(f32[2,1,16,1,2048]{4,0,3,2,1:T(2,128)S(1)} %get-tuple-element.89), channel_id=1, source_target_pairs={{0,1},{1,2},{2,3},{3,4},{4,5},{5,6},{6,7},{7,8},{8,9},{9,10},{10,1... | collective-permute-start | bytes 786440 | tf_op jit(solution)/shard_map/ppermute | solution.py:21
  320.9 9.2 %collective-permute-start.3 = (f32[2,1,16,1,2048]{4,0,3,2,1:T(2,128)S(1)}, f32[2,1,16,1,2048]{4,0,3,2,1:T(2,128)S(1)}, u32[]{:S(2)}, u32[]{:S(2)}) collective-permute-start(f32[2,1,16,1,2048]{4,0,3,2,1:T(2,128)S(1)} %get-tuple-element.90), channel_id=1, source_target_pairs={{1,0},{2,1},{3,2},{4,3},{5,4},{6,5},{7,6},{8,7},{9,8},{10,9},{11,1... | collective-permute-start | bytes 786440 | tf_op jit(solution)/shard_map/ppermute | solution.py:23
  359.2 11.4 %copy-start.6 = (f32[1,16,32,2048]{3,0,2,1:T(1,128)S(1)}, f32[1,16,32,2048]{3,0,2,1:T(1,128)}, u32[]{:S(2)}) copy-start(f32[1,16,32,2048]{3,0,2,1:T(1,128)} %copy-done.5) | copy-start | bytes 12582916
  359.2 11.4 %copy-start.12 = (f32[1,16,32,2048]{3,0,2,1:T(1,128)S(1)}, f32[1,16,32,2048]{3,0,2,1:T(1,128)}, u32[]{:S(2)}) copy-start(f32[1,16,32,2048]{3,0,2,1:T(1,128)} %slice.470) | copy-start | bytes 12582916
  359.2 11.4 %copy-start.14 = (f32[1,16,32,2048]{3,0,2,1:T(1,128)S(1)}, f32[1,16,32,2048]{3,0,2,1:T(1,128)}, u32[]{:S(2)}) copy-start(f32[1,16,32,2048]{3,0,2,1:T(1,128)} %slice.474) | copy-start | bytes 12582916
  509.7 6.8 %copy-start.2 = (f32[16,32,2048]{2,1,0:T(8,128)S(1)}, f32[16,32,2048]{2,1,0:T(8,128)}, u32[]{:S(2)}) copy-start(f32[16,32,2048]{2,1,0:T(8,128)} %all-gather.5.cloned.1.call-done) | copy-start | bytes 12582916
  540.6 9.7 %copy-start.10 = (f32[1,16,32,2048]{3,0,2,1:T(1,128)S(1)}, f32[1,16,32,2048]{3,0,2,1:T(1,128)}, u32[]{:S(2)}) copy-start(f32[1,16,32,2048]{3,0,2,1:T(1,128)} %copy-done.9) | copy-start | bytes 12582916
  (3 other events, 9.0 us)
Sparse Core Ops, SparseCore 0:
  181.4 92.0 all-gather.2
  417.6 92.0 all-gather.4
where the time goes:
time: 567 us; the launch traced here: 563 us
  waiting for transfers between devices  189 us (33%)
  other arithmetic  180 us (32%)
  matrix products  105 us (19%)
  local copies, waits for them, and re-layouts  60.2 us (11%)
  starting transfers between devices  14.5 us (3%)
  between operations  14.2 us (3%)
    all_gather x2, waiting for transfers between devices, local(): gathered = lax.all_gather(planes, 'tier', axis=0, tiled=True)  182 us
    add x2, other arithmetic, local(): heating_snapshot = heating_snapshot + step_dt * conduct(padded_t, padded_k)  88.8 us
    dot_general x16, matrix products, select_solve(): jnp.einsum('ij,jxc->ixc', matrices[which], planes, precision=lax.Precisio...  81.2 us
    another operation x3, other arithmetic, local(): joined = padded(jnp.stack([heating_snapshot, kappa]), (('tile', 3),), 1)  45.7 us
    dot_general x1, matrix products, local(): jnp.dot(onehot.reshape(-1, POWER_TILES), dissipation_per_patch[0], precis...  23.6 us
    mul x2, other arithmetic, conduct(): 0.5 * (kcell[..., 1:, :, :] + kcell[..., :-1, :, :])  22.8 us
    concatenate x2, other arithmetic, padded(): jnp.concatenate([lax.ppermute(tail, axis, [(i, (i + 1) % count) for i in...  16.1 us
    slice x2, local copies, waits for them, and re-layouts, conduct(): centre = padded_t[..., 1:-1, :]  15.8 us
  transfers between devices with their start and end apart: 6, of which 4 were waited for; matrix products, arithmetic and copies ran while one was open for 5% of the time, Pallas kernels for 0%

commit v1 on v0

--- a/solution.py
+++ b/solution.py
@@ -87,7 +87,9 @@
         heating_snapshot = heating_snapshot + step_dt * conduct(padded_t, padded_k)
         heating_snapshot = heating_snapshot.at[:, 0].add(step_dt * source)
         planes = jnp.stack([heating_snapshot[0, 0], heating_snapshot[0, -1]])
-        gathered = lax.all_gather(planes, "tier", axis=0, tiled=True)
+        gathered = jnp.concatenate(
+            lax.all_to_all(jnp.stack([planes] * lax.axis_size("tier")), "tier", 0, 0), axis=0
+        )
         own_rows = lax.dynamic_slice_in_dim(glue_sheet_reciprocal_operators, 2 * tier_index, 2, 1)
         updated = select_solve(own_rows, gathered, glue_zone_label)
         heating_snapshot = heating_snapshot.at[0, 0].set(updated[0]).at[0, -1].set(updated[1])

time: 567 us -> 476 us (0.84)
  waiting for transfers between devices: 189 us -> 61.2 us
  blocking collectives: 0 us -> 51.9 us
  matrix products: 105 us -> 67.4 us
  local copies, waits for them, and re-layouts: 60.2 us -> 87.5 us
  between operations: 14.2 us -> 0.75 us
  starting transfers between devices: 14.5 us -> 20.7 us
    all_gather x2 -> x0, waiting for transfers between devices: 182 us -> none  [local(): gathered = lax.all_gather(planes, 'tier', axis=0, tiled=True)]
    all_to_all x0 -> x1, waiting for transfers between devices: none -> 53.9 us  [local(): lax.all_to_all(jnp.stack([planes] * lax.axis_size('tier')), 'tier', 0, 0)]
    all_to_all x0 -> x1, blocking collectives: none -> 51.9 us  [local(): lax.all_to_all(jnp.stack([planes] * lax.axis_size('tier')), 'tier', 0, 0)]
    dot_general x16, matrix products: 81.2 us -> 43.8 us  [select_solve(): jnp.einsum('ij,jxc->ixc', matrices[which], planes, precision=lax.Precisio...]
    reshape x0 -> x2, local copies, waits for them, and re-layouts: none -> 12.3 us  [local(): jnp.concatenate(lax.all_to_all(jnp.stack([planes] * lax.axis_size('tier')...]
    all_to_all x0 -> x2, local copies, waits for them, and re-layouts: none -> 10.9 us  [local(): lax.all_to_all(jnp.stack([planes] * lax.axis_size('tier')), 'tier', 0, 0)]
    another operation x1 -> x3, local copies, waits for them, and re-layouts: 0.65 us -> 6.87 us  [the longest x2 6.3 us: local(): jnp.stack([planes] * lax.axis_size('tier'))]
  transfers between devices with their start and end apart: 6 -> 5, of which waited for: 4 -> 3; matrix products, arithmetic and copies ran while one was open for 5% -> 5% of each run, Pallas kernels for 0% -> 0%
where the time goes in v1:
time: 476 us; the launch traced here: 470 us
  other arithmetic  180 us (38%)
  local copies, waits for them, and re-layouts  87.5 us (18%)
  matrix products  67.4 us (14%)
  waiting for transfers between devices  61.2 us (13%)
  blocking collectives  51.9 us (11%)
  starting transfers between devices  20.7 us (4%)
    add x2, other arithmetic, local(): heating_snapshot = heating_snapshot + step_dt * conduct(padded_t, padded_k)  88.8 us
    all_to_all x1, waiting for transfers between devices, local(): lax.all_to_all(jnp.stack([planes] * lax.axis_size('tier')), 'tier', 0, 0)  53.9 us
    all_to_all x1, blocking collectives, local(): lax.all_to_all(jnp.stack([planes] * lax.axis_size('tier')), 'tier', 0, 0)  51.9 us
    another operation x3, other arithmetic, local(): joined = padded(jnp.stack([heating_snapshot, kappa]), (('tile', 3),), 1)  45.6 us
    dot_general x16, matrix products, select_solve(): jnp.einsum('ij,jxc->ixc', matrices[which], planes, precision=lax.Precisio...  43.8 us
    dot_general x1, matrix products, local(): jnp.dot(onehot.reshape(-1, POWER_TILES), dissipation_per_patch[0], precis...  23.6 us
    mul x2, other arithmetic, conduct(): 0.5 * (kcell[..., 1:, :, :] + kcell[..., :-1, :, :])  22.8 us
    concatenate x2, other arithmetic, padded(): jnp.concatenate([lax.ppermute(tail, axis, [(i, (i + 1) % count) for i in...  16.5 us
  transfers between devices with their start and end apart: 5, of which 3 were waited for; matrix products, arithmetic and copies ran while one was open for 5% of the time, Pallas kernels for 0%

profile of v1, /device:TPU:27, one launch (start us, length us, event | category | flops | bytes accessed | tf_op | source)
XLA Modules:
  0.0 469.7 jit_solution(9638974551437191721)
XLA Ops:
  2.0 5.0 %stack.18 = f32[1,1,16,32,2048]{4,0,3,2,1:T(1,128)S(1)} reshape(f32[1,16,32,2048]{3,2,1,0:T(8,128)} %param.19) | data formatting | bytes 8388608 | tf_op jit(solution)/shard_map/stack | solution.py:84
  7.0 44.7 %fusion.8 = f32[1,1,16,32,2048]{4,0,3,2,1:T(1,128)S(1)} fusion(s32[1,16,32,2048]{3,2,1,0:T(8,128)S(1)} %copy-done.16, f32[]{:T(128)} %bitcast.15, f32[]{:T(128)} %bitcast.14, f32[]{:T(128)} %bitcast.13, f32[]{:T(128)} %bitcast.12, f32[]{:T(128)} %bitcast.11, f32[]{:T(128)} %bitcast.10, f32[]{:T(128)} %bitcast.9, f32[]{:T(128)} %bitcast.8, f32[]{:T(128)} %bitcast.7, ...), kind=kLoop, calls=%fused_computation.33 | loop fusion | flops 33554432 | bytes 8388672 | tf_op jit(solution)/shard_map/stack | solution.py:84
  52.3 6.1 %collective-permute-start = (f32[2,1,16,1,2048]{4,0,3,2,1:T(2,128)S(1)}, f32[2,1,16,1,2048]{4,0,3,2,1:T(2,128)S(1)}, u32[]{:S(2)}, u32[]{:S(2)}) collective-permute-start(f32[2,1,16,1,2048]{4,0,3,2,1:T(2,128)S(1)} %get-tuple-element.77), channel_id=1, source_target_pairs={{0,1},{1,2},{2,3},{3,4},{4,5},{5,6},{6,7},{7,8},{8,9},{9,10},{10,1... | collective-permute-start | bytes 786440 | tf_op jit(solution)/shard_map/ppermute | solution.py:21
  60.5 23.6 %fusion.1 = f32[1,32,2048]{2,0,1:T(1,128)S(1)} fusion(s32[32,2048]{1,0:T(8,128)S(1)} %bitcast.130, f32[1,128]{1,0:T(1,128)S(1)} %copy-done.20), kind=kOutput, calls=%fused_computation.2 | convolution fusion | flops 109051904 | bytes 524800 | tf_op jit(solution)/shard_map/dot_general | solution.py:77
  84.2 8.0 %fusion.5 = f32[2,1,16,34,2048]{4,0,3,2,1:T(2,128)S(1)} fusion(f32[1,1,16,32,2048]{4,0,3,2,1:T(1,128)S(1)} %fusion.8, f32[2,1,16,1,2048]{4,0,3,2,1:T(2,128)S(1)} %collective-permute-done.1, f32[1,1,16,32,2048]{4,0,3,2,1:T(1,128)S(1)} %stack.18, f32[2,1,16,1,2048]{4,0,3,2,1:T(2,128)S(1)} %collective-permute-done), kind=kLoop, calls=%fused_computation.23 | loop fusion | flops 6684672 | bytes 17825792 | tf_op jit(solution)/shard_map/concatenate | solution.py:19
  92.2 7.9 %slice_bitcast_fusion.3 = (f32[1,16,34,2048]{3,0,2,1:T(1,128)S(1)}, f32[1,16,34,2048]{3,0,2,1:T(1,128)}) fusion(f32[2,1,16,34,2048]{4,0,3,2,1:T(2,128)S(1)} %fusion.5), kind=kLoop, calls=%fused_computation.32 | loop fusion | bytes 17825792 | tf_op jit(solution)/shard_map/squeeze | solution.py:86
  100.1 5.2 %slice.452 = f32[1,16,32,2048]{3,0,2,1:T(1,128)} slice(f32[1,16,34,2048]{3,0,2,1:T(1,128)S(1)} %get-tuple-element.83), slice={[0:1], [0:16], [1:33], [0:2048]} | slice | bytes 8388608 | tf_op jit(solution)/shard_map/slice | solution.py:38
  105.3 7.9 %slice.456 = f32[1,16,32,2048]{3,0,2,1:T(1,128)} slice(f32[1,16,34,2048]{3,0,2,1:T(1,128)} %get-tuple-element.84), slice={[0:1], [0:16], [1:33], [0:2048]} | slice | bytes 8388608 | tf_op jit(solution)/shard_map/slice | solution.py:37
  113.2 11.4 %fusion.21 = f32[1,15,32,2048]{3,0,2,1:T(1,128)S(1)} fusion(f32[1,16,34,2048]{3,0,2,1:T(1,128)} %get-tuple-element.84, f32[1,16,34,2048]{3,0,2,1:T(1,128)S(1)} %get-tuple-element.83), kind=kLoop, calls=%fused_computation.59 | loop fusion | flops 3932160 | bytes 19660800 | tf_op jit(solution)/shard_map/mul | solution.py:46
  124.6 46.4 %copy_add_fusion = f32[1,16,32,2048]{3,0,2,1:T(1,128)S(1)} fusion(f32[1,16,32,2048]{3,2,1,0:T(8,128)S(1)} %copy-done.11, f32[1,15,32,2048]{3,0,2,1:T(1,128)S(1)} %fusion.21, f32[1,16,32,2048]{3,0,2,1:T(1,128)S(1)} %copy-done.15, f32[1,16,32,2048]{3,0,2,1:T(1,128)S(1)} %copy-done.13, f32[1,16,34,2048]{3,0,2,1:T(1,128)} %get-tuple-element.84, ...), kind=kLoop, calls=%fused_computation.52 | loop fusion | flops 24117248 | bytes 37486592 | tf_op jit(solution)/shard_map/add | solution.py:87
  178.1 4.7 %all-to-all-start = ((f32[8,2,32,2048]{3,1,2,0:T(2,128)}), f32[8,2,32,2048]{3,1,2,0:T(2,128)}, u32[]{:S(2)}, u32[]{:S(2)}) async-start(f32[8,2,32,2048]{3,1,2,0:T(2,128)} %stack.22), calls=%async_computation | async-start | bytes 8388608 | tf_op jit(solution)/shard_map/all_to_all | solution.py:91
  184.5 53.9 %all-to-all-done = f32[8,2,32,2048]{3,1,2,0:T(2,128)} async-done(((f32[8,2,32,2048]{3,1,2,0:T(2,128)}), f32[8,2,32,2048]{3,1,2,0:T(2,128)}, u32[]{:S(2)}, u32[]{:S(2)}) %all-to-all-start) | async-done | bytes 4194336 | tf_op jit(solution)/shard_map/all_to_all | solution.py:91
  238.5 7.0 %copy.61 = f32[8,2,32,2048]{3,1,0,2:T(2,128)} copy(f32[8,2,32,2048]{3,1,2,0:T(2,128)} %all-to-all-done) | data formatting | bytes 8388608 | tf_op jit(solution)/shard_map/all_to_all | solution.py:91
  245.5 6.0 %reshape.256 = f32[16,32,2048]{2,0,1:T(8,128)} reshape(f32[8,2,32,2048]{3,1,0,2:T(2,128)} %copy.61) | data formatting | bytes 8388608 | tf_op jit(solution)/shard_map/reshape | solution.py:90
  276.1 5.9 %collective-permute-start.2 = (f32[2,1,16,1,2048]{4,0,3,2,1:T(2,128)S(1)}, f32[2,1,16,1,2048]{4,0,3,2,1:T(2,128)S(1)}, u32[]{:S(2)}, u32[]{:S(2)}) collective-permute-start(f32[2,1,16,1,2048]{4,0,3,2,1:T(2,128)S(1)} %get-tuple-element.89), channel_id=1, source_target_pairs={{0,1},{1,2},{2,3},{3,4},{4,5},{5,6},{6,7},{7,8},{8,9},{9,10},{10,1... | collective-permute-start | bytes 786440 | tf_op jit(solution)/shard_map/ppermute | solution.py:21
  285.3 5.9 %collective-permute-done.3 = f32[2,1,16,1,2048]{4,0,3,2,1:T(2,128)S(1)} collective-permute-done((f32[2,1,16,1,2048]{4,0,3,2,1:T(2,128)S(1)}, f32[2,1,16,1,2048]{4,0,3,2,1:T(2,128)S(1)}, u32[]{:S(2)}, u32[]{:S(2)}) %collective-permute-start.3) | collective-permute-done | bytes 262176 | tf_op jit(solution)/shard_map/ppermute | solution.py:23
  291.2 8.5 %fusion.7 = f32[2,1,16,34,2048]{4,0,3,2,1:T(2,128)S(1)} fusion(f32[1,1,16,32,2048]{4,0,3,2,1:T(1,128)S(1)} %copy-done.8, f32[2,1,16,1,2048]{4,0,3,2,1:T(2,128)S(1)} %collective-permute-done.3, f32[1,1,16,32,2048]{4,0,3,2,1:T(1,128)S(1)} %bitcast.129, f32[2,1,16,1,2048]{4,0,3,2,1:T(2,128)S(1)} %collective-permute-done.2), kind=kLoop, calls=%fused_computation.25 | loop fusion | flops 6684672 | bytes 17825792 | tf_op jit(solution)/shard_map/concatenate | solution.py:19
  299.7 7.9 %slice_bitcast_fusion.1 = (f32[1,16,34,2048]{3,0,2,1:T(1,128)S(1)}, f32[1,16,34,2048]{3,0,2,1:T(1,128)}) fusion(f32[2,1,16,34,2048]{4,0,3,2,1:T(2,128)S(1)} %fusion.7), kind=kLoop, calls=%fused_computation.30 | loop fusion | bytes 17825792 | tf_op jit(solution)/shard_map/squeeze | solution.py:86
  307.6 5.2 %slice.470 = f32[1,16,32,2048]{3,0,2,1:T(1,128)} slice(f32[1,16,34,2048]{3,0,2,1:T(1,128)S(1)} %get-tuple-element.81), slice={[0:1], [0:16], [1:33], [0:2048]} | slice | bytes 8388608 | tf_op jit(solution)/shard_map/slice | solution.py:38
  312.8 7.9 %slice.474 = f32[1,16,32,2048]{3,0,2,1:T(1,128)} slice(f32[1,16,34,2048]{3,0,2,1:T(1,128)} %get-tuple-element.82), slice={[0:1], [0:16], [1:33], [0:2048]} | slice | bytes 8388608 | tf_op jit(solution)/shard_map/slice | solution.py:37
  320.7 11.4 %fusion.19 = f32[1,15,32,2048]{3,0,2,1:T(1,128)S(1)} fusion(f32[1,16,34,2048]{3,0,2,1:T(1,128)} %get-tuple-element.82, f32[1,16,34,2048]{3,0,2,1:T(1,128)S(1)} %get-tuple-element.81), kind=kLoop, calls=%fused_computation.55 | loop fusion | flops 3932160 | bytes 19660800 | tf_op jit(solution)/shard_map/mul | solution.py:46
  332.1 42.4 %multiply_add_fusion = f32[1,16,32,2048]{3,0,2,1:T(1,128)S(1)} fusion(f32[1,16,32,2048]{3,0,2,1:T(1,128)S(1)} %copy-done.6, f32[1,15,32,2048]{3,0,2,1:T(1,128)S(1)} %fusion.19, f32[1,16,32,2048]{3,0,2,1:T(1,128)S(1)} %copy-done.14, f32[1,16,32,2048]{3,0,2,1:T(1,128)S(1)} %copy-done.12, f32[1,16,34,2048]{3,0,2,1:T(1,128)} %get-tuple-element.82, ...), kind=kLoop, calls=%fused_computation.53 | loop fusion | flops 24117248 | bytes 37486592 | tf_op jit(solution)/shard_map/add | solution.py:87
  379.6 51.9 %all_to_all.10 = f32[8,2,32,2048]{3,1,2,0:T(2,128)S(1)} all-to-all(f32[8,2,32,2048]{3,1,2,0:T(2,128)S(1)} %stack.52), channel_id=1, replica_groups=mesh['tier'=8,'tile'=16] {'tier'}, dimensions={0} | all-to-all | bytes 8388608 | tf_op jit(solution)/shard_map/all_to_all | solution.py:91
  435.4 6.3 %reshape.260 = f32[16,32,2048]{2,0,1:T(8,128)} reshape(f32[8,2,32,2048]{3,1,0,2:T(2,128)} %copy.62) | data formatting | bytes 8388608 | tf_op jit(solution)/shard_map/reshape | solution.py:90
  (85 shorter events, 77.8 us)
Async XLA Ops:
  0.0 251.5 %copy-start = (f32[8,16,16]{2,1,0:T(8,128)S(1)}, f32[8,16,16]{2,1,0:T(8,128)}, u32[]{:S(2)}) copy-start(f32[8,16,16]{2,1,0:T(8,128)} %param.25) | copy-start | bytes 24580
  1.9 5.0 %copy-start.16 = (s32[1,16,32,2048]{3,2,1,0:T(8,128)S(1)}, s32[1,16,32,2048]{3,2,1,0:T(8,128)}, u32[]{:S(2)}) copy-start(s32[1,16,32,2048]{3,2,1,0:T(8,128)} %param.20) | copy-start | bytes 12582916
  51.7 32.5 %copy-start.7 = (f32[1,1,16,32,2048]{4,0,3,2,1:T(1,128)}, f32[1,1,16,32,2048]{4,0,3,2,1:T(1,128)S(1)}, u32[]{:S(2)}) copy-start(f32[1,1,16,32,2048]{4,0,3,2,1:T(1,128)S(1)} %fusion.8) | copy-start | bytes 12582916
  51.7 8.8 %copy-start.19 = (s32[1,32,2048]{2,1,0:T(8,128)S(1)}, s32[1,32,2048]{2,1,0:T(8,128)}, u32[]{:S(2)}) copy-start(s32[1,32,2048]{2,1,0:T(8,128)} %param.22) | copy-start | bytes 786436
  51.7 8.8 %copy-start.20 = (f32[1,128]{1,0:T(1,128)S(1)}, f32[1,128]{1,0:T(1,128)}, u32[]{:S(2)}) copy-start(f32[1,128]{1,0:T(1,128)} %param.24) | copy-start | bytes 1540
  52.3 31.9 %collective-permute-start = (f32[2,1,16,1,2048]{4,0,3,2,1:T(2,128)S(1)}, f32[2,1,16,1,2048]{4,0,3,2,1:T(2,128)S(1)}, u32[]{:S(2)}, u32[]{:S(2)}) collective-permute-start(f32[2,1,16,1,2048]{4,0,3,2,1:T(2,128)S(1)} %get-tuple-element.77), channel_id=1, source_target_pairs={{0,1},{1,2},{2,3},{3,4},{4,5},{5,6},{6,7},{7,8},{8,9},{9,10},{10,1... | collective-permute-start | bytes 786440 | tf_op jit(solution)/shard_map/ppermute | solution.py:21
  58.4 25.8 %collective-permute-start.1 = (f32[2,1,16,1,2048]{4,0,3,2,1:T(2,128)S(1)}, f32[2,1,16,1,2048]{4,0,3,2,1:T(2,128)S(1)}, u32[]{:S(2)}, u32[]{:S(2)}) collective-permute-start(f32[2,1,16,1,2048]{4,0,3,2,1:T(2,128)S(1)} %get-tuple-element.91), channel_id=1, source_target_pairs={{1,0},{2,1},{3,2},{4,3},{5,4},{6,5},{7,6},{8,7},{9,8},{10,9},{11,1... | collective-permute-start | bytes 786440 | tf_op jit(solution)/shard_map/ppermute | solution.py:23
  113.1 11.4 %copy-start.11 = (f32[1,16,32,2048]{3,2,1,0:T(8,128)S(1)}, f32[1,16,32,2048]{3,2,1,0:T(8,128)}, u32[]{:S(2)}) copy-start(f32[1,16,32,2048]{3,2,1,0:T(8,128)} %param.19) | copy-start | bytes 12582916
  113.1 11.4 %copy-start.13 = (f32[1,16,32,2048]{3,0,2,1:T(1,128)S(1)}, f32[1,16,32,2048]{3,0,2,1:T(1,128)}, u32[]{:S(2)}) copy-start(f32[1,16,32,2048]{3,0,2,1:T(1,128)} %slice.452) | copy-start | bytes 12582916
  113.2 11.4 %copy-start.15 = (f32[1,16,32,2048]{3,0,2,1:T(1,128)S(1)}, f32[1,16,32,2048]{3,0,2,1:T(1,128)}, u32[]{:S(2)}) copy-start(f32[1,16,32,2048]{3,0,2,1:T(1,128)} %slice.456) | copy-start | bytes 12582916
  178.1 5.3 %copy-start.18 = (s32[4]{0:T(128)S(1)}, s32[4]{0:T(128)}, u32[]{:S(2)}) copy-start(s32[4]{0:T(128)} %constant.201.clone.1) | copy-start | bytes 52
  178.1 6.1 %copy-start.17 = (s32[32,2048]{1,0:T(8,128)S(1)}, s32[32,2048]{1,0:T(8,128)}, u32[]{:S(2)}) copy-start(s32[32,2048]{1,0:T(8,128)} %param.21) | copy-start | bytes 786436
  178.1 60.4 %all-to-all-start = ((f32[8,2,32,2048]{3,1,2,0:T(2,128)}), f32[8,2,32,2048]{3,1,2,0:T(2,128)}, u32[]{:S(2)}, u32[]{:S(2)}) async-start(f32[8,2,32,2048]{3,1,2,0:T(2,128)} %stack.22), calls=%async_computation | async-start | bytes 8388608 | tf_op jit(solution)/shard_map/all_to_all | solution.py:91
  251.5 4.6 copy-start.2
  268.4 5.1 %copy-start.4 = (f32[1,16,32,2048]{3,0,2,1:T(1,128)S(1)}, f32[1,16,32,2048]{3,0,2,1:T(1,128)}, u32[]{:S(2)}) copy-start(f32[1,16,32,2048]{3,0,2,1:T(1,128)} %copy-done.3) | copy-start | bytes 12582916
  273.5 17.7 %copy-start.8 = (f32[1,1,16,32,2048]{4,0,3,2,1:T(1,128)S(1)}, f32[1,1,16,32,2048]{4,0,3,2,1:T(1,128)}, u32[]{:S(2)}) copy-start(f32[1,1,16,32,2048]{4,0,3,2,1:T(1,128)} %copy-done.7) | copy-start | bytes 12582916
  275.7 31.9 %copy-start.5 = (f32[1,16,32,2048]{3,0,2,1:T(1,128)}, f32[1,16,32,2048]{3,0,2,1:T(1,128)S(1)}, u32[]{:S(2)}) copy-start(f32[1,16,32,2048]{3,0,2,1:T(1,128)S(1)} %fusion.39) | copy-start | bytes 12582916
  276.1 9.2 %collective-permute-start.2 = (f32[2,1,16,1,2048]{4,0,3,2,1:T(2,128)S(1)}, f32[2,1,16,1,2048]{4,0,3,2,1:T(2,128)S(1)}, u32[]{:S(2)}, u32[]{:S(2)}) collective-permute-start(f32[2,1,16,1,2048]{4,0,3,2,1:T(2,128)S(1)} %get-tuple-element.89), channel_id=1, source_target_pairs={{0,1},{1,2},{2,3},{3,4},{4,5},{5,6},{6,7},{7,8},{8,9},{9,10},{10,1... | collective-permute-start | bytes 786440 | tf_op jit(solution)/shard_map/ppermute | solution.py:21
  282.0 9.2 %collective-permute-start.3 = (f32[2,1,16,1,2048]{4,0,3,2,1:T(2,128)S(1)}, f32[2,1,16,1,2048]{4,0,3,2,1:T(2,128)S(1)}, u32[]{:S(2)}, u32[]{:S(2)}) collective-permute-start(f32[2,1,16,1,2048]{4,0,3,2,1:T(2,128)S(1)} %get-tuple-element.90), channel_id=1, source_target_pairs={{1,0},{2,1},{3,2},{4,3},{5,4},{6,5},{7,6},{8,7},{9,8},{10,9},{11,1... | collective-permute-start | bytes 786440 | tf_op jit(solution)/shard_map/ppermute | solution.py:23
  320.7 11.4 %copy-start.6 = (f32[1,16,32,2048]{3,0,2,1:T(1,128)S(1)}, f32[1,16,32,2048]{3,0,2,1:T(1,128)}, u32[]{:S(2)}) copy-start(f32[1,16,32,2048]{3,0,2,1:T(1,128)} %copy-done.5) | copy-start | bytes 12582916
  320.7 11.4 %copy-start.12 = (f32[1,16,32,2048]{3,0,2,1:T(1,128)S(1)}, f32[1,16,32,2048]{3,0,2,1:T(1,128)}, u32[]{:S(2)}) copy-start(f32[1,16,32,2048]{3,0,2,1:T(1,128)} %slice.470) | copy-start | bytes 12582916
  320.7 11.4 %copy-start.14 = (f32[1,16,32,2048]{3,0,2,1:T(1,128)S(1)}, f32[1,16,32,2048]{3,0,2,1:T(1,128)}, u32[]{:S(2)}) copy-start(f32[1,16,32,2048]{3,0,2,1:T(1,128)} %slice.474) | copy-start | bytes 12582916
  441.7 4.6 copy-start.1
  458.6 5.1 %copy-start.10 = (f32[1,16,32,2048]{3,0,2,1:T(1,128)S(1)}, f32[1,16,32,2048]{3,0,2,1:T(1,128)}, u32[]{:S(2)}) copy-start(f32[1,16,32,2048]{3,0,2,1:T(1,128)} %copy-done.9) | copy-start | bytes 12582916
  (2 other events, 4.0 us)
